TPU v7x, 1024 devices: a whole 4x4x32 slice. The times are simulated.
1024 devices in a mesh: ctx: 128 (over y, z), tp: 8 (over x, core).
Axes of the slice: x: 4, y: 4, z: 32, core: 2. Of those that a mesh axis runs over, the one named last changes fastest.
Arguments:
- tokens: bfloat16 [32768, 2048], P('ctx'), may hold values from -6 to 6
- w_query: bfloat16 [2048, 4096], P(None, 'tp'), may hold values from -0.125 to 0.125
- w_key: bfloat16 [2048, 512], replicated, may hold values from -0.125 to 0.125
- w_value: bfloat16 [2048, 512], replicated, may hold values from -0.125 to 0.125
- w_out: bfloat16 [4096, 2048], P('tp'), may hold values from -0.09375 to 0.09375
- query_gain: float32 [128], replicated, may hold values from 0.5 to 2
- key_gain: float32 [128], replicated, may hold values from 0.5 to 2
- doc_lengths: int32 [256], replicated, may hold values from 1 to 4096, as said below
Outputs:
- layer_out: bfloat16 [32768, 2048], P('ctx', 'tp')
Inputs may be any that keep to these rules, and one draw needn't show every extreme that they name: `doc_lengths`: the lengths sum to 32768; the second-to-last document has exactly 4096 tokens and the last one exactly 128.
All inputs are finite; a program needn't handle non-finite values.
Results may differ from a plain program's by a relative error of at most 0.014.
Values may be sent and summed in bfloat16 or wider, within the bound.
No kernel may reach another device: no remote copies, remote signals or barrier semaphores. Data moves between devices by JAX's collectives and lax.ppermute only.
A program may use at most 32 MiB of HBM per device.

v0:
```python
import jax
import jax.numpy as jnp
from jax import lax
from jax.sharding import PartitionSpec as P

H = 32
KVH = 4
HD = 128


EPSILON = 1e-06
ROPE_BASE = 1000000.0
NEGATIVE = -1e30


def passed_along(block, axis, distance):
    devices = range(lax.axis_size(axis))
    route = [(i - distance, i) for i in devices if i - distance in devices]
    return lax.ppermute(block, axis, route)


def doc_starts(positions, doc_lengths):
    doc_ends = jnp.cumsum(doc_lengths)
    before = doc_ends[None, :] <= positions[:, None]
    return jnp.sum(jnp.where(before, doc_lengths[None, :], 0), axis=1)


def norm_rotate(inputs, gain_vec, offsets):
    full_width = inputs.shape[-1]
    half_width = full_width // 2
    inv_norm = lax.rsqrt(jnp.mean(inputs * inputs, axis=-1, keepdims=True) + EPSILON)
    normed = inputs * inv_norm * gain_vec
    frequency = ROPE_BASE ** (-2.0 * jnp.arange(half_width, dtype=jnp.float32) / full_width)
    angles = offsets[:, None] * frequency[None, :]
    cosine = jnp.cos(angles)[:, None, :]
    sine_part = jnp.sin(angles)[:, None, :]
    first_half = normed[..., :half_width]
    second_half = normed[..., half_width:]
    return jnp.concatenate(
        [
            first_half * cosine - second_half * sine_part,
            second_half * cosine + first_half * sine_part,
        ],
        axis=-1,
    )


def local(tokens, w_query, w_key, w_value, w_out, query_gain, key_gain, doc_lengths):
    row_count = tokens.shape[0]
    head_count = w_query.shape[1] // HD
    tp_rank = lax.axis_index("tp")
    my_block = lax.axis_index("ctx")
    reach_blocks = min(16, lax.axis_size("ctx") // 2)
    kv_head = tp_rank * head_count // (H // KVH)
    key_cols = lax.dynamic_slice_in_dim(w_key, kv_head * HD, HD, 1)
    value_cols = lax.dynamic_slice_in_dim(w_value, kv_head * HD, HD, 1)
    positions = my_block * row_count + jnp.arange(row_count, dtype=jnp.int32)
    starts_local = doc_starts(positions, doc_lengths)
    offsets = (positions - starts_local).astype(jnp.float32)
    query_proj = jnp.dot(tokens, w_query, preferred_element_type=jnp.float32).reshape(
        row_count, head_count, HD
    )
    queries = (
        norm_rotate(query_proj, query_gain, offsets)
        .astype(jnp.bfloat16)
        .reshape(row_count * head_count, HD)
    )
    key_proj = jnp.dot(tokens, key_cols, preferred_element_type=jnp.float32).reshape(
        row_count, 1, HD
    )
    keys_local = (
        norm_rotate(key_proj, key_gain, offsets).reshape(row_count, HD).astype(jnp.bfloat16)
    )
    values_local = jnp.dot(tokens, value_cols, preferred_element_type=jnp.float32).astype(
        jnp.bfloat16
    )
    key_value = jnp.stack([keys_local, values_local])
    query_pos = jnp.repeat(positions, head_count)
    query_start = jnp.repeat(starts_local, head_count)

    def attend(softmax_state, kv_block, key_block):
        row_peak, row_total, weighted = softmax_state
        key_pos = key_block * row_count + jnp.arange(row_count, dtype=jnp.int32)
        scores = lax.dot_general(
            queries, kv_block[0], (((1,), (1,)), ((), ())), preferred_element_type=jnp.float32
        ) * HD ** (-0.5)
        visible = (key_pos[None, :] <= query_pos[:, None]) & (
            key_pos[None, :] >= query_start[:, None]
        )
        new_peak = jnp.maximum(row_peak, jnp.max(jnp.where(visible, scores, NEGATIVE), axis=1))
        weights = jnp.where(visible, jnp.exp(scores - new_peak[:, None]), 0.0)
        factor = jnp.exp(row_peak - new_peak)
        row_total = row_total * factor + jnp.sum(weights, axis=1)
        weighted = weighted * factor[:, None] + jnp.dot(
            weights.astype(jnp.bfloat16), kv_block[1], preferred_element_type=jnp.float32
        )
        return (new_peak, row_total, weighted)

    def use_tile(softmax_state, kv_block, key_block):
        return attend(softmax_state, kv_block, key_block)

    query_rows = row_count * head_count
    initial = (
        jnp.full((query_rows,), NEGATIVE, jnp.float32),
        jnp.zeros((query_rows,), jnp.float32),
        jnp.zeros((query_rows, HD), jnp.float32),
    )
    softmax_state = attend(initial, key_value, my_block)

    def advance(offset, carry):
        moving, state_in = carry
        moving = passed_along(moving, "ctx", 1)
        return (moving, use_tile(state_in, moving, my_block - offset - 1))

    _, softmax_state = lax.fori_loop(0, reach_blocks, advance, (key_value, softmax_state))
    attended = (
        (softmax_state[2] / softmax_state[1][:, None])
        .astype(jnp.bfloat16)
        .reshape(row_count, head_count * HD)
    )
    head_term = jnp.dot(attended, w_out, preferred_element_type=jnp.float32)
    return lax.psum_scatter(head_term.astype(jnp.bfloat16), "tp", scatter_dimension=1, tiled=True)


def solution(mesh):
    return jax.shard_map(
        local,
        mesh=mesh,
        in_specs=(P("ctx", None), P(None, "tp"), P(), P(), P("tp", None), P(), P(), P()),
        out_specs=P("ctx", "tp"),
        check_vma=False,
    )
```

profile of v0, /device:TPU:7, one launch (start us, length us, event | category | flops | bytes accessed | tf_op | source)
XLA Modules:
  0.0 241.3 jit_solution(3805675334189409604)
XLA Ops:
  6.6 1.1 reduce-window.9
  8.0 0.9 select_reduce_fusion.2
  8.9 2.6 %fusion.37 = f32[256,512]{1,0:T(8,128)S(1)} fusion(bf16[256,2048]{1,0:T(8,128)(2,1)} %param.10, bf16[2048,512]{1,0:T(8,128)(2,1)} %param.11), kind=kOutput, calls=%fused_computation.74 | convolution fusion | flops 536870912 | bytes 3670016 | tf_op jit(solution)/shard_map/dot_general | solution.py:60
  12.1 1.9 multiply_reduce_fusion.1
  14.0 0.5 multiply_cosine_fusion
  15.8 0.5 subtract_convert_fusion
  16.5 0.4 select_reduce_fusion.1
  17.6 1.5 convolution_convert_fusion.1
  19.1 0.5 convolution_add_fusion.1
  19.8 130.8 %while.22 = (s32[]{:T(128)}, bf16[2,256,128]{2,1,0:T(8,128)(2,1)S(1)}, f32[1024]{0:T(1024)S(1)}, f32[1024]{0:T(1024)S(1)}, f32[1024,128]{1,0:T(8,128)S(1)}, /*in...) while((s32[]{:T(128)}, ...), condition=%wide.region_10.11_spmd.clone, body=%wide.region_7.10_spmd.clone.sunk | while | flops 139200768 | bytes 5494981 | solution.py:115
  19.8 3.5 %collective-permute-start = (bf16[2,256,128]{2,1,0:T(8,128)(2,1)S(1)}, bf16[2,256,128]{2,1,0:T(8,128)(2,1)S(1)}, u32[]{:S(2)}, u32[]{:S(2)}) collective-permute-start(bf16[2,256,128]{2,1,0:T(8,128)(2,1)S(1)} %get-tuple-element.406), channel_id=1, source_target_pairs={{0,8},{8,16},{16,24},{24,32},{32,40},{40,48},{48,56},{56,64},{64,7... | collective-permute-start | bytes 393224 | tf_op jit(solution)/shard_map/while/body/eval_jaxpr/ppermute | solution.py:19
  23.8 1.7 collective-permute-done
  25.5 0.4 select_reduce_fusion.4
  26.2 0.6 convolution_add_fusion.3
  26.9 4.1 %collective-permute-start = (bf16[2,256,128]{2,1,0:T(8,128)(2,1)S(1)}, bf16[2,256,128]{2,1,0:T(8,128)(2,1)S(1)}, u32[]{:S(2)}, u32[]{:S(2)}) collective-permute-start(bf16[2,256,128]{2,1,0:T(8,128)(2,1)S(1)} %get-tuple-element.406), channel_id=1, source_target_pairs={{0,8},{8,16},{16,24},{24,32},{32,40},{40,48},{48,56},{56,64},{64,7... | collective-permute-start | bytes 393224 | tf_op jit(solution)/shard_map/while/body/eval_jaxpr/ppermute | solution.py:19
  31.4 1.5 collective-permute-done
  33.7 0.6 convolution_add_fusion.3
  34.3 3.8 %collective-permute-start = (bf16[2,256,128]{2,1,0:T(8,128)(2,1)S(1)}, bf16[2,256,128]{2,1,0:T(8,128)(2,1)S(1)}, u32[]{:S(2)}, u32[]{:S(2)}) collective-permute-start(bf16[2,256,128]{2,1,0:T(8,128)(2,1)S(1)} %get-tuple-element.406), channel_id=1, source_target_pairs={{0,8},{8,16},{16,24},{24,32},{32,40},{40,48},{48,56},{56,64},{64,7... | collective-permute-start | bytes 393224 | tf_op jit(solution)/shard_map/while/body/eval_jaxpr/ppermute | solution.py:19
  38.5 1.5 collective-permute-done
  40.8 0.6 convolution_add_fusion.3
  41.4 4.0 %collective-permute-start = (bf16[2,256,128]{2,1,0:T(8,128)(2,1)S(1)}, bf16[2,256,128]{2,1,0:T(8,128)(2,1)S(1)}, u32[]{:S(2)}, u32[]{:S(2)}) collective-permute-start(bf16[2,256,128]{2,1,0:T(8,128)(2,1)S(1)} %get-tuple-element.406), channel_id=1, source_target_pairs={{0,8},{8,16},{16,24},{24,32},{32,40},{40,48},{48,56},{56,64},{64,7... | collective-permute-start | bytes 393224 | tf_op jit(solution)/shard_map/while/body/eval_jaxpr/ppermute | solution.py:19
  45.8 1.5 collective-permute-done
  48.0 0.6 convolution_add_fusion.3
  48.6 5.3 %collective-permute-start = (bf16[2,256,128]{2,1,0:T(8,128)(2,1)S(1)}, bf16[2,256,128]{2,1,0:T(8,128)(2,1)S(1)}, u32[]{:S(2)}, u32[]{:S(2)}) collective-permute-start(bf16[2,256,128]{2,1,0:T(8,128)(2,1)S(1)} %get-tuple-element.406), channel_id=1, source_target_pairs={{0,8},{8,16},{16,24},{24,32},{32,40},{40,48},{48,56},{56,64},{64,7... | collective-permute-start | bytes 393224 | tf_op jit(solution)/shard_map/while/body/eval_jaxpr/ppermute | solution.py:19
  54.4 1.5 collective-permute-done
  56.7 0.6 convolution_add_fusion.3
  57.3 5.0 %collective-permute-start = (bf16[2,256,128]{2,1,0:T(8,128)(2,1)S(1)}, bf16[2,256,128]{2,1,0:T(8,128)(2,1)S(1)}, u32[]{:S(2)}, u32[]{:S(2)}) collective-permute-start(bf16[2,256,128]{2,1,0:T(8,128)(2,1)S(1)} %get-tuple-element.406), channel_id=1, source_target_pairs={{0,8},{8,16},{16,24},{24,32},{32,40},{40,48},{48,56},{56,64},{64,7... | collective-permute-start | bytes 393224 | tf_op jit(solution)/shard_map/while/body/eval_jaxpr/ppermute | solution.py:19
  62.7 1.5 collective-permute-done
  65.0 0.6 convolution_add_fusion.3
  65.6 5.0 %collective-permute-start = (bf16[2,256,128]{2,1,0:T(8,128)(2,1)S(1)}, bf16[2,256,128]{2,1,0:T(8,128)(2,1)S(1)}, u32[]{:S(2)}, u32[]{:S(2)}) collective-permute-start(bf16[2,256,128]{2,1,0:T(8,128)(2,1)S(1)} %get-tuple-element.406), channel_id=1, source_target_pairs={{0,8},{8,16},{16,24},{24,32},{32,40},{40,48},{48,56},{56,64},{64,7... | collective-permute-start | bytes 393224 | tf_op jit(solution)/shard_map/while/body/eval_jaxpr/ppermute | solution.py:19
  71.1 1.5 collective-permute-done
  72.5 0.4 select_reduce_fusion.4
  73.3 0.6 convolution_add_fusion.3
  73.9 5.0 %collective-permute-start = (bf16[2,256,128]{2,1,0:T(8,128)(2,1)S(1)}, bf16[2,256,128]{2,1,0:T(8,128)(2,1)S(1)}, u32[]{:S(2)}, u32[]{:S(2)}) collective-permute-start(bf16[2,256,128]{2,1,0:T(8,128)(2,1)S(1)} %get-tuple-element.406), channel_id=1, source_target_pairs={{0,8},{8,16},{16,24},{24,32},{32,40},{40,48},{48,56},{56,64},{64,7... | collective-permute-start | bytes 393224 | tf_op jit(solution)/shard_map/while/body/eval_jaxpr/ppermute | solution.py:19
  79.4 1.5 collective-permute-done
  81.6 0.6 convolution_add_fusion.3
  82.2 5.2 %collective-permute-start = (bf16[2,256,128]{2,1,0:T(8,128)(2,1)S(1)}, bf16[2,256,128]{2,1,0:T(8,128)(2,1)S(1)}, u32[]{:S(2)}, u32[]{:S(2)}) collective-permute-start(bf16[2,256,128]{2,1,0:T(8,128)(2,1)S(1)} %get-tuple-element.406), channel_id=1, source_target_pairs={{0,8},{8,16},{16,24},{24,32},{32,40},{40,48},{48,56},{56,64},{64,7... | collective-permute-start | bytes 393224 | tf_op jit(solution)/shard_map/while/body/eval_jaxpr/ppermute | solution.py:19
  87.9 2.5 %collective-permute-done = bf16[2,256,128]{2,1,0:T(8,128)(2,1)S(1)} collective-permute-done((bf16[2,256,128]{2,1,0:T(8,128)(2,1)S(1)}, bf16[2,256,128]{2,1,0:T(8,128)(2,1)S(1)}, u32[]{:S(2)}, u32[]{:S(2)}) %collective-permute-start) | collective-permute-done | bytes 131104 | tf_op jit(solution)/shard_map/while/body/eval_jaxpr/ppermute | solution.py:19
  91.2 0.6 convolution_add_fusion.3
  91.8 5.6 %collective-permute-start = (bf16[2,256,128]{2,1,0:T(8,128)(2,1)S(1)}, bf16[2,256,128]{2,1,0:T(8,128)(2,1)S(1)}, u32[]{:S(2)}, u32[]{:S(2)}) collective-permute-start(bf16[2,256,128]{2,1,0:T(8,128)(2,1)S(1)} %get-tuple-element.406), channel_id=1, source_target_pairs={{0,8},{8,16},{16,24},{24,32},{32,40},{40,48},{48,56},{56,64},{64,7... | collective-permute-start | bytes 393224 | tf_op jit(solution)/shard_map/while/body/eval_jaxpr/ppermute | solution.py:19
  97.9 2.0 collective-permute-done
  99.8 0.4 select_reduce_fusion.4
  100.6 0.6 convolution_add_fusion.3
  101.2 4.7 %collective-permute-start = (bf16[2,256,128]{2,1,0:T(8,128)(2,1)S(1)}, bf16[2,256,128]{2,1,0:T(8,128)(2,1)S(1)}, u32[]{:S(2)}, u32[]{:S(2)}) collective-permute-start(bf16[2,256,128]{2,1,0:T(8,128)(2,1)S(1)} %get-tuple-element.406), channel_id=1, source_target_pairs={{0,8},{8,16},{16,24},{24,32},{32,40},{40,48},{48,56},{56,64},{64,7... | collective-permute-start | bytes 393224 | tf_op jit(solution)/shard_map/while/body/eval_jaxpr/ppermute | solution.py:19
  106.4 1.5 collective-permute-done
  108.6 0.6 convolution_add_fusion.3
  109.2 4.5 %collective-permute-start = (bf16[2,256,128]{2,1,0:T(8,128)(2,1)S(1)}, bf16[2,256,128]{2,1,0:T(8,128)(2,1)S(1)}, u32[]{:S(2)}, u32[]{:S(2)}) collective-permute-start(bf16[2,256,128]{2,1,0:T(8,128)(2,1)S(1)} %get-tuple-element.406), channel_id=1, source_target_pairs={{0,8},{8,16},{16,24},{24,32},{32,40},{40,48},{48,56},{56,64},{64,7... | collective-permute-start | bytes 393224 | tf_op jit(solution)/shard_map/while/body/eval_jaxpr/ppermute | solution.py:19
  114.2 1.5 collective-permute-done
  116.4 0.6 convolution_add_fusion.3
  117.1 5.3 %collective-permute-start = (bf16[2,256,128]{2,1,0:T(8,128)(2,1)S(1)}, bf16[2,256,128]{2,1,0:T(8,128)(2,1)S(1)}, u32[]{:S(2)}, u32[]{:S(2)}) collective-permute-start(bf16[2,256,128]{2,1,0:T(8,128)(2,1)S(1)} %get-tuple-element.406), channel_id=1, source_target_pairs={{0,8},{8,16},{16,24},{24,32},{32,40},{40,48},{48,56},{56,64},{64,7... | collective-permute-start | bytes 393224 | tf_op jit(solution)/shard_map/while/body/eval_jaxpr/ppermute | solution.py:19
  122.8 1.5 collective-permute-done
  125.1 0.6 convolution_add_fusion.3
  125.7 5.0 %collective-permute-start = (bf16[2,256,128]{2,1,0:T(8,128)(2,1)S(1)}, bf16[2,256,128]{2,1,0:T(8,128)(2,1)S(1)}, u32[]{:S(2)}, u32[]{:S(2)}) collective-permute-start(bf16[2,256,128]{2,1,0:T(8,128)(2,1)S(1)} %get-tuple-element.406), channel_id=1, source_target_pairs={{0,8},{8,16},{16,24},{24,32},{32,40},{40,48},{48,56},{56,64},{64,7... | collective-permute-start | bytes 393224 | tf_op jit(solution)/shard_map/while/body/eval_jaxpr/ppermute | solution.py:19
  131.1 1.5 collective-permute-done
  133.4 0.6 convolution_add_fusion.3
  134.0 5.0 %collective-permute-start = (bf16[2,256,128]{2,1,0:T(8,128)(2,1)S(1)}, bf16[2,256,128]{2,1,0:T(8,128)(2,1)S(1)}, u32[]{:S(2)}, u32[]{:S(2)}) collective-permute-start(bf16[2,256,128]{2,1,0:T(8,128)(2,1)S(1)} %get-tuple-element.406), channel_id=1, source_target_pairs={{0,8},{8,16},{16,24},{24,32},{32,40},{40,48},{48,56},{56,64},{64,7... | collective-permute-start | bytes 393224 | tf_op jit(solution)/shard_map/while/body/eval_jaxpr/ppermute | solution.py:19
  139.5 1.5 collective-permute-done
  140.9 0.4 select_reduce_fusion.4
  141.7 0.6 convolution_add_fusion.3
  142.3 5.0 %collective-permute-start = (bf16[2,256,128]{2,1,0:T(8,128)(2,1)S(1)}, bf16[2,256,128]{2,1,0:T(8,128)(2,1)S(1)}, u32[]{:S(2)}, u32[]{:S(2)}) collective-permute-start(bf16[2,256,128]{2,1,0:T(8,128)(2,1)S(1)} %get-tuple-element.406), channel_id=1, source_target_pairs={{0,8},{8,16},{16,24},{24,32},{32,40},{40,48},{48,56},{56,64},{64,7... | collective-permute-start | bytes 393224 | tf_op jit(solution)/shard_map/while/body/eval_jaxpr/ppermute | solution.py:19
  147.8 1.5 collective-permute-done
  150.0 0.6 convolution_add_fusion.3
  151.0 1.7 convolution_convert_fusion
  152.7 81.7 %reduce-scatter.2.cloned.1.call-done = bf16[256,256]{1,0:T(8,128)(2,1)} async-done(((bf16[256,2048]{1,0:T(8,128)(2,1)}), bf16[256,256]{1,0:T(8,128)(2,1)}) %reduce-scatter.2.cloned.1.call-update) | async-done | bytes 131088 | tf_op jit(solution)/shard_map/reduce_scatter | solution.py:122
  (209 shorter events, 20.1 us)
Async XLA Ops:
  6.5 144.5 %copy-start = (bf16[512,2048]{1,0:T(8,128)(2,1)S(1)}, bf16[512,2048]{1,0:T(8,128)(2,1)}, u32[]{:S(2)}) copy-start(bf16[512,2048]{1,0:T(8,128)(2,1)} %param.14) | copy-start | bytes 6291460
  6.5 227.9 %reduce-scatter.2.cloned.1.call-start = ((), (), s32[]{:S(2)}) async-start(), calls=%async_computation.1 | async-start | bytes 1179648 | tf_op jit(solution)/shard_map/reduce_scatter | solution.py:122
  11.5 3.1 %copy-start.2 = (f32[128]{0:T(128)S(1)}, f32[128]{0:T(128)}, u32[]{:S(2)}) copy-start(f32[128]{0:T(128)} %param.16) | copy-start | bytes 1540
  11.7 3.7 %copy-start.3 = (f32[128]{0:T(128)S(1)}, f32[128]{0:T(128)}, u32[]{:S(2)}) copy-start(f32[128]{0:T(128)} %param.15) | copy-start | bytes 1540
  16.3 1.2 copy-start.1
  19.8 5.7 %collective-permute-start = (bf16[2,256,128]{2,1,0:T(8,128)(2,1)S(1)}, bf16[2,256,128]{2,1,0:T(8,128)(2,1)S(1)}, u32[]{:S(2)}, u32[]{:S(2)}) collective-permute-start(bf16[2,256,128]{2,1,0:T(8,128)(2,1)S(1)} %get-tuple-element.406), channel_id=1, source_target_pairs={{0,8},{8,16},{16,24},{24,32},{32,40},{40,48},{48,56},{56,64},{64,7... | collective-permute-start | bytes 393224 | tf_op jit(solution)/shard_map/while/body/eval_jaxpr/ppermute | solution.py:19
  26.9 6.0 %collective-permute-start = (bf16[2,256,128]{2,1,0:T(8,128)(2,1)S(1)}, bf16[2,256,128]{2,1,0:T(8,128)(2,1)S(1)}, u32[]{:S(2)}, u32[]{:S(2)}) collective-permute-start(bf16[2,256,128]{2,1,0:T(8,128)(2,1)S(1)} %get-tuple-element.406), channel_id=1, source_target_pairs={{0,8},{8,16},{16,24},{24,32},{32,40},{40,48},{48,56},{56,64},{64,7... | collective-permute-start | bytes 393224 | tf_op jit(solution)/shard_map/while/body/eval_jaxpr/ppermute | solution.py:19
  34.3 5.7 %collective-permute-start = (bf16[2,256,128]{2,1,0:T(8,128)(2,1)S(1)}, bf16[2,256,128]{2,1,0:T(8,128)(2,1)S(1)}, u32[]{:S(2)}, u32[]{:S(2)}) collective-permute-start(bf16[2,256,128]{2,1,0:T(8,128)(2,1)S(1)} %get-tuple-element.406), channel_id=1, source_target_pairs={{0,8},{8,16},{16,24},{24,32},{32,40},{40,48},{48,56},{56,64},{64,7... | collective-permute-start | bytes 393224 | tf_op jit(solution)/shard_map/while/body/eval_jaxpr/ppermute | solution.py:19
  41.4 5.9 %collective-permute-start = (bf16[2,256,128]{2,1,0:T(8,128)(2,1)S(1)}, bf16[2,256,128]{2,1,0:T(8,128)(2,1)S(1)}, u32[]{:S(2)}, u32[]{:S(2)}) collective-permute-start(bf16[2,256,128]{2,1,0:T(8,128)(2,1)S(1)} %get-tuple-element.406), channel_id=1, source_target_pairs={{0,8},{8,16},{16,24},{24,32},{32,40},{40,48},{48,56},{56,64},{64,7... | collective-permute-start | bytes 393224 | tf_op jit(solution)/shard_map/while/body/eval_jaxpr/ppermute | solution.py:19
  48.6 7.3 %collective-permute-start = (bf16[2,256,128]{2,1,0:T(8,128)(2,1)S(1)}, bf16[2,256,128]{2,1,0:T(8,128)(2,1)S(1)}, u32[]{:S(2)}, u32[]{:S(2)}) collective-permute-start(bf16[2,256,128]{2,1,0:T(8,128)(2,1)S(1)} %get-tuple-element.406), channel_id=1, source_target_pairs={{0,8},{8,16},{16,24},{24,32},{32,40},{40,48},{48,56},{56,64},{64,7... | collective-permute-start | bytes 393224 | tf_op jit(solution)/shard_map/while/body/eval_jaxpr/ppermute | solution.py:19
  57.3 6.9 %collective-permute-start = (bf16[2,256,128]{2,1,0:T(8,128)(2,1)S(1)}, bf16[2,256,128]{2,1,0:T(8,128)(2,1)S(1)}, u32[]{:S(2)}, u32[]{:S(2)}) collective-permute-start(bf16[2,256,128]{2,1,0:T(8,128)(2,1)S(1)} %get-tuple-element.406), channel_id=1, source_target_pairs={{0,8},{8,16},{16,24},{24,32},{32,40},{40,48},{48,56},{56,64},{64,7... | collective-permute-start | bytes 393224 | tf_op jit(solution)/shard_map/while/body/eval_jaxpr/ppermute | solution.py:19
  65.6 6.9 %collective-permute-start = (bf16[2,256,128]{2,1,0:T(8,128)(2,1)S(1)}, bf16[2,256,128]{2,1,0:T(8,128)(2,1)S(1)}, u32[]{:S(2)}, u32[]{:S(2)}) collective-permute-start(bf16[2,256,128]{2,1,0:T(8,128)(2,1)S(1)} %get-tuple-element.406), channel_id=1, source_target_pairs={{0,8},{8,16},{16,24},{24,32},{32,40},{40,48},{48,56},{56,64},{64,7... | collective-permute-start | bytes 393224 | tf_op jit(solution)/shard_map/while/body/eval_jaxpr/ppermute | solution.py:19
  73.9 6.9 %collective-permute-start = (bf16[2,256,128]{2,1,0:T(8,128)(2,1)S(1)}, bf16[2,256,128]{2,1,0:T(8,128)(2,1)S(1)}, u32[]{:S(2)}, u32[]{:S(2)}) collective-permute-start(bf16[2,256,128]{2,1,0:T(8,128)(2,1)S(1)} %get-tuple-element.406), channel_id=1, source_target_pairs={{0,8},{8,16},{16,24},{24,32},{32,40},{40,48},{48,56},{56,64},{64,7... | collective-permute-start | bytes 393224 | tf_op jit(solution)/shard_map/while/body/eval_jaxpr/ppermute | solution.py:19
  82.2 8.2 %collective-permute-start = (bf16[2,256,128]{2,1,0:T(8,128)(2,1)S(1)}, bf16[2,256,128]{2,1,0:T(8,128)(2,1)S(1)}, u32[]{:S(2)}, u32[]{:S(2)}) collective-permute-start(bf16[2,256,128]{2,1,0:T(8,128)(2,1)S(1)} %get-tuple-element.406), channel_id=1, source_target_pairs={{0,8},{8,16},{16,24},{24,32},{32,40},{40,48},{48,56},{56,64},{64,7... | collective-permute-start | bytes 393224 | tf_op jit(solution)/shard_map/while/body/eval_jaxpr/ppermute | solution.py:19
  91.8 8.0 %collective-permute-start = (bf16[2,256,128]{2,1,0:T(8,128)(2,1)S(1)}, bf16[2,256,128]{2,1,0:T(8,128)(2,1)S(1)}, u32[]{:S(2)}, u32[]{:S(2)}) collective-permute-start(bf16[2,256,128]{2,1,0:T(8,128)(2,1)S(1)} %get-tuple-element.406), channel_id=1, source_target_pairs={{0,8},{8,16},{16,24},{24,32},{32,40},{40,48},{48,56},{56,64},{64,7... | collective-permute-start | bytes 393224 | tf_op jit(solution)/shard_map/while/body/eval_jaxpr/ppermute | solution.py:19
  101.2 6.6 %collective-permute-start = (bf16[2,256,128]{2,1,0:T(8,128)(2,1)S(1)}, bf16[2,256,128]{2,1,0:T(8,128)(2,1)S(1)}, u32[]{:S(2)}, u32[]{:S(2)}) collective-permute-start(bf16[2,256,128]{2,1,0:T(8,128)(2,1)S(1)} %get-tuple-element.406), channel_id=1, source_target_pairs={{0,8},{8,16},{16,24},{24,32},{32,40},{40,48},{48,56},{56,64},{64,7... | collective-permute-start | bytes 393224 | tf_op jit(solution)/shard_map/while/body/eval_jaxpr/ppermute | solution.py:19
  109.2 6.4 %collective-permute-start = (bf16[2,256,128]{2,1,0:T(8,128)(2,1)S(1)}, bf16[2,256,128]{2,1,0:T(8,128)(2,1)S(1)}, u32[]{:S(2)}, u32[]{:S(2)}) collective-permute-start(bf16[2,256,128]{2,1,0:T(8,128)(2,1)S(1)} %get-tuple-element.406), channel_id=1, source_target_pairs={{0,8},{8,16},{16,24},{24,32},{32,40},{40,48},{48,56},{56,64},{64,7... | collective-permute-start | bytes 393224 | tf_op jit(solution)/shard_map/while/body/eval_jaxpr/ppermute | solution.py:19
  117.1 7.3 %collective-permute-start = (bf16[2,256,128]{2,1,0:T(8,128)(2,1)S(1)}, bf16[2,256,128]{2,1,0:T(8,128)(2,1)S(1)}, u32[]{:S(2)}, u32[]{:S(2)}) collective-permute-start(bf16[2,256,128]{2,1,0:T(8,128)(2,1)S(1)} %get-tuple-element.406), channel_id=1, source_target_pairs={{0,8},{8,16},{16,24},{24,32},{32,40},{40,48},{48,56},{56,64},{64,7... | collective-permute-start | bytes 393224 | tf_op jit(solution)/shard_map/while/body/eval_jaxpr/ppermute | solution.py:19
  125.7 6.9 %collective-permute-start = (bf16[2,256,128]{2,1,0:T(8,128)(2,1)S(1)}, bf16[2,256,128]{2,1,0:T(8,128)(2,1)S(1)}, u32[]{:S(2)}, u32[]{:S(2)}) collective-permute-start(bf16[2,256,128]{2,1,0:T(8,128)(2,1)S(1)} %get-tuple-element.406), channel_id=1, source_target_pairs={{0,8},{8,16},{16,24},{24,32},{32,40},{40,48},{48,56},{56,64},{64,7... | collective-permute-start | bytes 393224 | tf_op jit(solution)/shard_map/while/body/eval_jaxpr/ppermute | solution.py:19
  134.0 6.9 %collective-permute-start = (bf16[2,256,128]{2,1,0:T(8,128)(2,1)S(1)}, bf16[2,256,128]{2,1,0:T(8,128)(2,1)S(1)}, u32[]{:S(2)}, u32[]{:S(2)}) collective-permute-start(bf16[2,256,128]{2,1,0:T(8,128)(2,1)S(1)} %get-tuple-element.406), channel_id=1, source_target_pairs={{0,8},{8,16},{16,24},{24,32},{32,40},{40,48},{48,56},{56,64},{64,7... | collective-permute-start | bytes 393224 | tf_op jit(solution)/shard_map/while/body/eval_jaxpr/ppermute | solution.py:19
  142.3 6.9 %collective-permute-start = (bf16[2,256,128]{2,1,0:T(8,128)(2,1)S(1)}, bf16[2,256,128]{2,1,0:T(8,128)(2,1)S(1)}, u32[]{:S(2)}, u32[]{:S(2)}) collective-permute-start(bf16[2,256,128]{2,1,0:T(8,128)(2,1)S(1)} %get-tuple-element.406), channel_id=1, source_target_pairs={{0,8},{8,16},{16,24},{24,32},{32,40},{40,48},{48,56},{56,64},{64,7... | collective-permute-start | bytes 393224 | tf_op jit(solution)/shard_map/while/body/eval_jaxpr/ppermute | solution.py:19
Sparse Core Ops, SparseCore 0:
  152.9 81.5 reduce-scatter.1
where the time goes:
time: 242 us; the launch traced here: 241 us
  waiting for transfers between devices  107 us (44%)
  starting transfers between devices  76 us (31%)
  matrix products  24.3 us (10%)
  between operations  13.7 us (6%)
  other arithmetic  10.3 us (4%)
  local copies, waits for them, and re-layouts  8.24 us (3%)
    reduce_scatter x1, waiting for transfers between devices, local(): lax.psum_scatter(head_term.astype(jnp.bfloat16), 'tp', scatter_dimension=...  81.7 us
    ppermute x16, starting transfers between devices, passed_along(): return lax.ppermute(block, axis, route)  76 us
    ppermute x16, waiting for transfers between devices, passed_along(): return lax.ppermute(block, axis, route)  25.3 us
    dot_general x17, matrix products, attend(): jnp.dot(weights.astype(jnp.bfloat16), kv_block[1], preferred_element_type...  10.1 us
    dot_general x17, matrix products, attend(): lax.dot_general(queries, kv_block[0], (((1,), (1,)), ((), ())), preferred...  6.52 us
    reduce_sum x17, other arithmetic, attend(): row_total = row_total * factor + jnp.sum(weights, axis=1)  5.32 us
  transfers between devices with their start and end apart: 17, of which 17 were waited for; matrix products, arithmetic and copies ran while one was open for 3% of the time, Pallas kernels for 0%

commit v1 on v0

v1 whole, which is shorter than its diff:
```python
import functools

import jax
import jax.numpy as jnp
from jax import lax
from jax.experimental import pallas as pl
from jax.experimental.pallas import tpu as pltpu
from jax.sharding import Mesh, PartitionSpec as P

H = 32
KVH = 4
HD = 128
REACH = 16
LINE = 4
EPSILON = 1e-06
ROPE_BASE = 1000000.0
LOG2E = 1.4426950408889634

CTX = ("y", "zh", "zl")
TP = ("x", "c")
VMEM = pltpu.VMEM


def doc_starts(positions, doc_lengths):
    doc_ends = jnp.cumsum(doc_lengths)
    before = doc_ends[None, :] <= positions[:, None]
    return jnp.sum(jnp.where(before, doc_lengths[None, :], 0), axis=1)


def norm_rotate(u, gain, cosine, sine):
    inv = lax.rsqrt(jnp.mean(u * u, axis=-1, keepdims=True) + EPSILON)
    w = u * inv * gain
    return w * cosine + pltpu.roll(w, HD // 2, 1) * sine


def kv_body(info, tokens, w_key, w_value, gain, cosine, sine, out):
    @pl.when(info[1] == 0)
    def _():
        u = jnp.dot(tokens[...], w_key[...], preferred_element_type=jnp.float32)
        out[...] = norm_rotate(u, gain[...], cosine[...], sine[...]).astype(out.dtype)

    @pl.when(info[1] != 0)
    def _():
        u = jnp.dot(tokens[...], w_value[...], preferred_element_type=jnp.float32)
        out[...] = u.astype(out.dtype)


def project_kv(info, tokens, w_key, w_value, gain, cosine, sine):
    rows, width = tokens.shape
    head = pl.BlockSpec((width, HD), lambda i, s: (0, s[0]))

    def whole(a):
        return pl.BlockSpec(a.shape, lambda i, s: (0,) * a.ndim)

    return pl.pallas_call(
        kv_body,
        out_shape=jax.ShapeDtypeStruct((rows, HD), jnp.bfloat16),
        grid_spec=pltpu.PrefetchScalarGridSpec(
            num_scalar_prefetch=1,
            grid=(1,),
            in_specs=[whole(tokens), head, head, whole(gain), whole(cosine), whole(sine)],
            out_specs=pl.BlockSpec((rows, HD), lambda i, s: (0, 0)),
        ),
        cost_estimate=pl.CostEstimate(
            flops=2 * rows * width * HD, bytes_accessed=2 * rows * width, transcendentals=0
        ),
        name="project_kv",
    )(info, tokens, w_key, w_value, gain, cosine, sine)


def q_body(heads, tokens, w_query, gain, cosine, sine, out):
    u = jnp.dot(tokens[...], w_query[...], preferred_element_type=jnp.float32)
    for h in range(heads):
        part = u[:, h * HD : (h + 1) * HD]
        out[h] = norm_rotate(part, gain[...], cosine[...], sine[...]).astype(out.dtype)


def project_q(tokens, w_query, gain, cosine, sine):
    rows, width = tokens.shape
    heads = w_query.shape[1] // HD
    return pl.pallas_call(
        functools.partial(q_body, heads),
        out_shape=jax.ShapeDtypeStruct((heads, rows, HD), jnp.bfloat16),
        in_specs=[pl.BlockSpec(memory_space=VMEM)] * 5,
        out_specs=pl.BlockSpec(memory_space=VMEM),
        cost_estimate=pl.CostEstimate(
            flops=2 * rows * width * heads * HD, bytes_accessed=6 * rows * width, transcendentals=0
        ),
        name="project_q",
    )(tokens, w_query, gain, cosine, sine)


def add_block(heads, queries, key, value, total, weighted, mask):
    for h in range(heads):
        scores = lax.dot_general(
            queries[h], key, (((1,), (1,)), ((), ())), preferred_element_type=jnp.float32
        )
        weights = jnp.exp2(scores * (HD**-0.5 * LOG2E))
        if mask is not None:
            weights = weights * mask[...]
        total[h] += weights[:, :HD] + weights[:, HD:]
        weighted[h] += jnp.dot(
            weights.astype(jnp.bfloat16), value, preferred_element_type=jnp.float32
        )


def attend_body(heads, info, queries, kv, starts, w_out, out, total, weighted, mask, attended):
    rows = queries.shape[1]
    block, first, last = info[0], info[1], info[2]
    total[...] = jnp.zeros_like(total)
    weighted[...] = jnp.zeros_like(weighted)
    group = block // LINE

    def step(b, carry):
        back = group - b // LINE
        place = (b % LINE) * 2
        key, value = kv[place, back], kv[place + 1, back]
        whole = (b < block) & (b * rows >= last)

        @pl.when(whole)
        def _():
            add_block(heads, queries, key, value, total, weighted, None)

        @pl.when(jnp.logical_not(whole))
        def _():
            key_pos = b * rows + lax.broadcasted_iota(jnp.int32, (rows, rows), 1)
            query_pos = block * rows + lax.broadcasted_iota(jnp.int32, (rows, rows), 0)
            visible = (key_pos <= query_pos) & (key_pos >= starts[...])
            mask[...] = jnp.where(visible, 1.0, 0.0)
            add_block(heads, queries, key, value, total, weighted, mask)

        return carry

    lax.fori_loop(first // rows, block + 1, step, 0)
    for h in range(heads):
        sums = jnp.sum(total[h], axis=1, keepdims=True)
        attended[:, h * HD : (h + 1) * HD] = (weighted[h] / sums).astype(attended.dtype)
    out[...] = jnp.dot(
        attended[...], w_out[...], preferred_element_type=jnp.float32
    ).astype(out.dtype)


def attend(info, queries, kv, starts, w_out):
    heads, rows, _ = queries.shape
    return pl.pallas_call(
        functools.partial(attend_body, heads),
        out_shape=jax.ShapeDtypeStruct((rows, w_out.shape[1]), jnp.bfloat16),
        in_specs=[pl.BlockSpec(memory_space=pltpu.SMEM)] + [pl.BlockSpec(memory_space=VMEM)] * 4,
        out_specs=pl.BlockSpec(memory_space=VMEM),
        scratch_shapes=[
            VMEM((heads, rows, HD), jnp.float32),
            VMEM((heads, rows, HD), jnp.float32),
            VMEM((rows, rows), jnp.float32),
            VMEM((rows, heads * HD), jnp.bfloat16),
        ],
        cost_estimate=pl.CostEstimate(
            flops=(REACH + 1) * 4 * heads * rows * rows * HD, bytes_accessed=4 << 20, transcendentals=0
        ),
        name="attend",
    )(info, queries, kv, starts, w_out)


def local(tokens, w_query, w_key, w_value, w_out, query_gain, key_gain, doc_lengths):
    rows = tokens.shape[0]
    heads = w_query.shape[1] // HD
    tp_rank = lax.axis_index(TP)
    block = lax.axis_index(CTX)
    core = lax.axis_index("c")
    kv_head = tp_rank * heads // (H // KVH)
    positions = block * rows + jnp.arange(rows, dtype=jnp.int32)
    starts = doc_starts(positions, doc_lengths)
    offsets = (positions - starts).astype(jnp.float32)
    half = HD // 2
    frequency = ROPE_BASE ** (-2.0 * jnp.arange(half, dtype=jnp.float32) / HD)
    angles = offsets[:, None] * frequency[None, :]
    cosine = jnp.cos(angles)
    sine = jnp.sin(angles)
    cosine = jnp.concatenate([cosine, cosine], axis=1)
    sine = jnp.concatenate([-sine, sine], axis=1)
    info = jnp.stack([kv_head, core]).astype(jnp.int32)
    part = project_kv(info, tokens, w_key, w_value, key_gain[None], cosine, sine)
    queries = project_q(tokens, w_query, query_gain[None], cosine, sine)

    groups = lax.axis_size("y") * lax.axis_size("zh")
    onward = [(i, (i + 1) % groups) for i in range(groups)]
    parts = [part]
    for _ in range(REACH // LINE):
        parts.append(lax.ppermute(parts[-1], ("y", "zh"), onward))
    kv = lax.all_gather(jnp.stack(parts), ("zl", "c"), axis=0)

    info = jnp.stack([block, starts[0], starts[rows - 1]]).astype(jnp.int32)
    head_term = attend(info, queries, kv, starts[:, None], w_out)
    return lax.psum_scatter(head_term, TP, scatter_dimension=1, tiled=True)


def solution(mesh):
    ctx, tp = mesh.shape["ctx"], mesh.shape["tp"]
    y = max(1, ctx // 32)
    devices = mesh.devices.reshape(y, ctx // (y * LINE), LINE, tp // 2, 2)
    fine = Mesh(devices, CTX + TP)
    return jax.shard_map(
        local,
        mesh=fine,
        in_specs=(P(CTX, None), P(None, TP), P(), P(), P(TP, None), P(), P(), P()),
        out_specs=P(CTX, TP),
        check_vma=False,
    )
```

time: 242 us -> 194 us (0.80); the launches traced: 241 us -> 196 us
  starting transfers between devices: 76 us -> 14.6 us
  waiting for transfers between devices: 107 us -> 147 us
  matrix products: 24.3 us -> 0 us
  Pallas kernels: 0 us -> 12 us
  local copies, waits for them, and re-layouts: 8.24 us -> 3.17 us
  other arithmetic: 10.3 us -> 5.82 us
    ppermute x16 -> x4, starting transfers between devices: 76 us -> 14.5 us  [local(): parts.append(lax.ppermute(parts[-1], ('y', 'zh'), onward))]
    all_gather x0 -> x1, waiting for transfers between devices: none -> 45 us  [local(): kv = lax.all_gather(jnp.stack(parts), ('zl', 'c'), axis=0)]
    dot_general x38 -> x0, matrix products: 24.3 us -> none  [the longest x17 10.1 us: attend(): jnp.dot(weights.astype(jnp.bfloat16), kv_block[1], preferred_element_type...]
    reduce_scatter x1, waiting for transfers between devices: 81.7 us -> 60 us  [local(): return lax.psum_scatter(head_term, TP, scatter_dimension=1, tiled=True)]
    ppermute x16 -> x4, waiting for transfers between devices: 25.3 us -> 41.9 us  [local(): parts.append(lax.ppermute(parts[-1], ('y', 'zh'), onward))]
    pallas_call x0 -> x3, Pallas kernels: none -> 12 us  [the longest x1 5.1 us: attend(): pl.pallas_call(functools.partial(attend_body, heads), out_shape=jax.Shape...]
    reduce_sum x18 -> x0, other arithmetic: 5.67 us -> none  [the longest x17 5.32 us: attend(): row_total = row_total * factor + jnp.sum(weights, axis=1)]
    broadcast_in_dim x34 -> x0, local copies, waits for them, and re-layouts: 3 us -> none  [the longest x17 1.5 us: local(): query_pos = jnp.repeat(positions, head_count)]
  transfers between devices with their start and end apart: 17 -> 6, of which waited for: 17 -> 6; matrix products, arithmetic and copies ran while one was open for 3% -> 2% of each run, Pallas kernels for 0% -> 2%
where the time goes in v1:
time: 194 us; the launch traced here: 196 us
  waiting for transfers between devices  147 us (76%)
  starting transfers between devices  14.6 us (8%)
  between operations  13.5 us (7%)
  Pallas kernels  12 us (6%)
  other arithmetic  5.82 us (3%)
  local copies, waits for them, and re-layouts  3.17 us (2%)
    reduce_scatter x1, waiting for transfers between devices, local(): return lax.psum_scatter(head_term, TP, scatter_dimension=1, tiled=True)  60 us
    all_gather x1, waiting for transfers between devices, local(): kv = lax.all_gather(jnp.stack(parts), ('zl', 'c'), axis=0)  45 us
    ppermute x4, waiting for transfers between devices, local(): parts.append(lax.ppermute(parts[-1], ('y', 'zh'), onward))  41.9 us
    ppermute x4, starting transfers between devices, local(): parts.append(lax.ppermute(parts[-1], ('y', 'zh'), onward))  14.5 us
    pallas_call x1, Pallas kernels, attend(): pl.pallas_call(functools.partial(attend_body, heads), out_shape=jax.Shape...  5.1 us
  transfers between devices with their start and end apart: 6, of which 6 were waited for; matrix products, arithmetic and copies ran while one was open for 2% of the time, Pallas kernels for 2%

profile of v1, /device:TPU:7, one launch (start us, length us, event | category | flops | bytes accessed | tf_op | source)
XLA Modules:
  0.0 196.0 jit_solution(14540597688293761613)
XLA Ops:
  6.5 0.0 all-gather.3.cloned.1.call-start
  6.6 1.0 reduce-window.9
  7.5 0.1 slice.13
  7.7 0.1 slice_reduce_fusion
  7.8 0.1 add_bitcast_fusion
  7.9 0.9 select_reduce_fusion
  8.7 0.6 pad_add_fusion.1.info
  9.4 0.5 fusion
  9.9 0.8 pad_maximum_fusion
  10.7 3.3 %project_kv.1 = bf16[256,128]{1,0:T(8,128)(2,1)} custom-call(s32[2]{0:T(128)} %pad_add_fusion.1.info, bf16[256,2048]{1,0:T(8,128)(2,1)} %tokens.3, bf16[2048,512]{1,0:T(8,128)(2,1)} %w_key.1, bf16[2048,512]{1,0:T(8,128)(2,1)} %w_value.1, f32[1,128]{1,0:T(1,128)} %bitcast.22, f32[256,128]{1,0:T(8,128)} %get-tuple-element.10.cosine, ...), custom_call_target="tpu_custom_call" | custom-call | flops 134217728 | bytes 1048576 | tf_op jit(solution)/shard_map/project_kv/pallas_call | solution.py:55
  14.1 8.8 %collective-permute-start = (bf16[256,128]{1,0:T(8,128)(2,1)}, bf16[256,128]{1,0:T(8,128)(2,1)S(1)}, u32[]{:S(2)}, u32[]{:S(2)}) collective-permute-start(bf16[256,128]{1,0:T(8,128)(2,1)} %project_kv.1), channel_id=1, source_target_pairs={{0,32},{32,64},{64,96},{96,128},{128,160},{160,192},{192,224},{224... | collective-permute-start | bytes 196616 | tf_op jit(solution)/shard_map/ppermute | solution.py:188
  22.9 0.9 bitcast_dynamic-update-slice_fusion.4
  23.7 14.7 %collective-permute-done = bf16[256,128]{1,0:T(8,128)(2,1)S(1)} collective-permute-done((bf16[256,128]{1,0:T(8,128)(2,1)}, bf16[256,128]{1,0:T(8,128)(2,1)S(1)}, u32[]{:S(2)}, u32[]{:S(2)}) %collective-permute-start) | collective-permute-done | bytes 65568 | tf_op jit(solution)/shard_map/ppermute | solution.py:188
  38.4 1.9 collective-permute-start.1
  40.3 9.1 %collective-permute-done.1 = bf16[256,128]{1,0:T(8,128)(2,1)S(1)} collective-permute-done((bf16[256,128]{1,0:T(8,128)(2,1)S(1)}, bf16[256,128]{1,0:T(8,128)(2,1)S(1)}, u32[]{:S(2)}, u32[]{:S(2)}) %collective-permute-start.1) | collective-permute-done | bytes 65568 | tf_op jit(solution)/shard_map/ppermute | solution.py:188
  49.4 1.9 collective-permute-start.2
  51.4 9.1 %collective-permute-done.2 = bf16[256,128]{1,0:T(8,128)(2,1)S(1)} collective-permute-done((bf16[256,128]{1,0:T(8,128)(2,1)S(1)}, bf16[256,128]{1,0:T(8,128)(2,1)S(1)}, u32[]{:S(2)}, u32[]{:S(2)}) %collective-permute-start.2) | collective-permute-done | bytes 65568 | tf_op jit(solution)/shard_map/ppermute | solution.py:188
  60.4 1.9 collective-permute-start.3
  62.4 9.1 %collective-permute-done.3 = bf16[256,128]{1,0:T(8,128)(2,1)S(1)} collective-permute-done((bf16[256,128]{1,0:T(8,128)(2,1)S(1)}, bf16[256,128]{1,0:T(8,128)(2,1)S(1)}, u32[]{:S(2)}, u32[]{:S(2)}) %collective-permute-start.3) | collective-permute-done | bytes 65568 | tf_op jit(solution)/shard_map/ppermute | solution.py:188
  71.5 0.0 copy-start
  71.5 0.7 copy-done
  72.2 0.0 all-gather.3.cloned.1.call-update
  72.2 0.0 reduce-scatter.2.cloned.1.call-start
  72.3 0.8 copy.11.starts
  73.0 3.6 %project_q.1.queries = bf16[4,256,128]{2,1,0:T(8,128)(2,1)} custom-call(bf16[256,2048]{1,0:T(8,128)(2,1)} %tokens.3, bf16[2048,512]{1,0:T(8,128)(2,1)} %w_query.1, f32[1,128]{1,0:T(1,128)} %bitcast.23, f32[256,128]{1,0:T(8,128)} %get-tuple-element.10.cosine, f32[256,128]{1,0:T(8,128)} %get-tuple-element.11.sine), custom_call_target="tpu_custom_call" | custom-call | flops 536870912 | bytes 3145728 | tf_op jit(solution)/shard_map/project_q/pallas_call | solution.py:81
  76.6 0.6 fusion.1
  77.2 1.9 pad_add_fusion.info
  79.1 45.0 %all-gather.3.cloned.1.call-done = bf16[40,256,128]{2,1,0:T(8,128)(2,1)} async-done(((bf16[5,256,128]{2,1,0:T(8,128)(2,1)}), bf16[40,256,128]{2,1,0:T(8,128)(2,1)}) %all-gather.3.cloned.1.call-update) | async-done | bytes 2621456 | tf_op jit(solution)/shard_map/all_gather | solution.py:189
  124.0 5.1 %attend.1 = bf16[256,2048]{1,0:T(8,128)(2,1)} custom-call(s32[3]{0:T(128)} %pad_add_fusion.info, bf16[4,256,128]{2,1,0:T(8,128)(2,1)} %project_q.1.queries, bf16[8,5,256,128]{3,2,1,0:T(8,128)(2,1)} %bitcast.24, s32[256,1]{1,0:T(8,128)} %copy.11.starts, bf16[512,2048]{1,0:T(8,128)(2,1)} %w_out.1), custom_call_target="tpu_custom_call" | custom-call | flops 2281701376 | bytes 4194304 | tf_op jit(solution)/shard_map/attend/pallas_call | solution.py:145
  129.1 0.0 reduce-scatter.2.cloned.1.call-update
  129.1 60.0 %reduce-scatter.2.cloned.1.call-done = bf16[256,256]{1,0:T(8,128)(2,1)} async-done(((bf16[256,2048]{1,0:T(8,128)(2,1)}), bf16[256,256]{1,0:T(8,128)(2,1)}) %reduce-scatter.2.cloned.1.call-update) | async-done | bytes 131088 | tf_op jit(solution)/shard_map/reduce_scatter | solution.py:193
  (8 shorter events, 0.1 us)
Async XLA Ops:
  6.5 117.5 %all-gather.3.cloned.1.call-start = ((), (), s32[]{:S(2)}) async-start(), calls=%async_computation.2 | async-start | bytes 2949120 | tf_op jit(solution)/shard_map/all_gather | solution.py:189
  14.1 24.3 %collective-permute-start = (bf16[256,128]{1,0:T(8,128)(2,1)}, bf16[256,128]{1,0:T(8,128)(2,1)S(1)}, u32[]{:S(2)}, u32[]{:S(2)}) collective-permute-start(bf16[256,128]{1,0:T(8,128)(2,1)} %project_kv.1), channel_id=1, source_target_pairs={{0,32},{32,64},{64,96},{96,128},{128,160},{160,192},{192,224},{224... | collective-permute-start | bytes 196616 | tf_op jit(solution)/shard_map/ppermute | solution.py:188
  38.4 11.0 %collective-permute-start.1 = (bf16[256,128]{1,0:T(8,128)(2,1)S(1)}, bf16[256,128]{1,0:T(8,128)(2,1)S(1)}, u32[]{:S(2)}, u32[]{:S(2)}) collective-permute-start(bf16[256,128]{1,0:T(8,128)(2,1)S(1)} %collective-permute-done), channel_id=1, source_target_pairs={{0,32},{32,64},{64,96},{96,128},{128,160},{160,192},{192,224},{224... | collective-permute-start | bytes 196616 | tf_op jit(solution)/shard_map/ppermute | solution.py:188
  49.4 11.0 %collective-permute-start.2 = (bf16[256,128]{1,0:T(8,128)(2,1)S(1)}, bf16[256,128]{1,0:T(8,128)(2,1)S(1)}, u32[]{:S(2)}, u32[]{:S(2)}) collective-permute-start(bf16[256,128]{1,0:T(8,128)(2,1)S(1)} %collective-permute-done.1), channel_id=1, source_target_pairs={{0,32},{32,64},{64,96},{96,128},{128,160},{160,192},{192,224},{224... | collective-permute-start | bytes 196616 | tf_op jit(solution)/shard_map/ppermute | solution.py:188
  60.4 11.0 %collective-permute-start.3 = (bf16[256,128]{1,0:T(8,128)(2,1)S(1)}, bf16[256,128]{1,0:T(8,128)(2,1)S(1)}, u32[]{:S(2)}, u32[]{:S(2)}) collective-permute-start(bf16[256,128]{1,0:T(8,128)(2,1)S(1)} %collective-permute-done.2), channel_id=1, source_target_pairs={{0,32},{32,64},{64,96},{96,128},{128,160},{160,192},{192,224},{224... | collective-permute-start | bytes 196616 | tf_op jit(solution)/shard_map/ppermute | solution.py:188
  71.5 0.7 copy-start
  72.2 116.9 %reduce-scatter.2.cloned.1.call-start = ((), (), s32[]{:S(2)}) async-start(), calls=%async_computation.1 | async-start | bytes 1179648 | tf_op jit(solution)/shard_map/reduce_scatter | solution.py:193
Sparse Core Ops, SparseCore 0:
  72.3 51.6 all-gather.2
  129.3 59.7 reduce-scatter.1
